TPU v7x, 32 devices: a whole 2x2x4 slice. The times are simulated.
32 devices in a mesh: space: 4 (over x, core), tile: 8 (over z, y).
Axes of the slice: x: 2, y: 2, z: 4, core: 2. Of those that a mesh axis runs over, the one named last changes fastest.
Arguments:
- atom_feat: bfloat16 [512, 128, 128], P(('space', 'tile')), may hold values from -6 to 6
- atom_pos: bfloat16 [512, 3, 128], P(('space', 'tile')), may hold values from 0 to 4
- atom_counts: int32 [512], P(('space', 'tile')), may hold values from 32 to 128
- atom_nbrs: int32 [512, 4], P(('space', 'tile')), may hold values from 0 to 511, as said below
- probe_pos: float32 [64, 3, 512], P(('space', 'tile')), may hold values from 0 to 4
- probe_target: float32 [64, 512], P(('space', 'tile')), may hold values from -6 to 6
- tile_blocks: int32 [64, 8], P(('space', 'tile')), may hold values from 0 to 511, as said below
- atom_filter: bfloat16 [128, 1024], replicated, may hold values from -0.5 to 0.5
- probe_filter: bfloat16 [128, 1024], replicated, may hold values from -0.5 to 0.5
- mix_weight: bfloat16 [128, 128], replicated, may hold values from -0.5 to 0.5
- readout: float32 [128], replicated, may hold values from -0.5 to 0.5
Outputs:
- density: float32 [64, 512], P(('space', 'tile'))
- atom_filter_grad: float32 [128, 1024], replicated
- probe_filter_grad: float32 [128, 1024], replicated
- mix_grad: float32 [128, 128], replicated
- readout_grad: float32 [128], replicated
Inputs may be any that keep to these rules, and one draw needn't show every extreme that they name: `atom_nbrs`: block g lies on device g // 16 in the order space then tile. The 4 neighbours of a block lie on devices of the same tile index whose space index differs by at most one, cyclically: the first one lower, the second one higher, the third the same; they need not be distinct. `tile_blocks`: the 8 blocks of a tile are distinct and lie on devices of the tile's own space index. The tiles of one device read at most 4 distinct blocks from any one device, and exactly 4 from some device.
All inputs are finite; a program needn't handle non-finite values.
Results may differ from a plain program's by a relative error of at most 0.0061.
Values may be sent and summed in bfloat16 or wider, within the bound.
A program may use at most 64 MiB of HBM per device.

v0:
```python
import jax
import jax.numpy as jnp
from jax import lax
from jax.sharding import PartitionSpec as P

CUTOFF = 6.0
SPACING = 0.75
SPREAD = 0.75


def with_halo(block, sides, width):
    for axis, dim in sides:
        count = lax.axis_size(axis)
        forward = [(i, i + 1) for i in range(count - 1)]
        forward.append((count - 1, 0))
        backward = [(target, source) for source, target in forward]
        low = lax.ppermute(
            lax.slice_in_dim(block, block.shape[dim] - width, None, axis=dim), axis, forward
        )
        high = lax.ppermute(lax.slice_in_dim(block, 0, width, axis=dim), axis, backward)
        block = jnp.concatenate([low, block, high], axis=dim)
    return block


def silu_slope(values):
    sigmoid_part = jax.nn.sigmoid(values)
    return sigmoid_part * (1.0 + values * (1.0 - sigmoid_part))


def radial(source, target, factor, filters):
    square = jnp.zeros((source.shape[1], target.shape[1]), jnp.float32)
    for component in range(3):
        offset = source[component][:, None] - target[component][None, :]
        square = square + offset * offset
    distance = jnp.sqrt(square + 0.01)
    envelope = jnp.where(distance < CUTOFF, 0.5 * (jnp.cos(jnp.pi * distance / CUTOFF) + 1.0), 0.0)
    centers = jnp.arange(filters).astype(jnp.float32) * SPACING
    shifted = (distance[None] - centers[:, None, None]) / SPREAD
    return (jnp.exp(-shifted * shifted) * (envelope * factor)[None]).astype(jnp.bfloat16)


def body(
    atom_feat,
    atom_pos,
    atom_counts,
    atom_nbrs,
    probe_pos,
    probe_target,
    tile_blocks,
    atom_filter,
    probe_filter,
    mix_weight,
    readout,
):
    highest = lax.Precision.HIGHEST
    blocks_dev, channels, atom_width = atom_feat.shape
    tiles_dev, reads_tile = tile_blocks.shape
    probe_count = probe_pos.shape[2]
    filters = atom_filter.shape[1] // channels
    nbr_count = atom_nbrs.shape[1]
    tile_peers = lax.axis_size("tile")
    space_count = lax.axis_size("space")
    space_here = lax.axis_index("space")
    atom_mask = (jnp.arange(atom_width)[None, :] < atom_counts[:, None]).astype(jnp.float32)
    masked_feat = (atom_feat.astype(jnp.float32) * atom_mask[:, None, :]).astype(jnp.bfloat16)
    packed_rows = jnp.concatenate([masked_feat, atom_pos], axis=1)
    around_rows = with_halo(packed_rows, (("space", 0),), blocks_dev)
    side_index = (atom_nbrs // (tile_peers * blocks_dev) - space_here + 1) % space_count
    source_rows = side_index * blocks_dev + atom_nbrs % blocks_dev
    neighbour_rows = jnp.take(around_rows, source_rows.reshape(-1), axis=0).reshape(
        blocks_dev, nbr_count, channels + 3, atom_width
    )
    atom_scale = (nbr_count * atom_width) ** (-0.5)

    def atom_block(inputs):
        picked_rows, own_pos, own_feat, own_mask = inputs
        source_feat = picked_rows[:, :channels]
        source_where = picked_rows[:, channels:].astype(jnp.float32)
        target_where = own_pos.astype(jnp.float32)
        kernel_rows = jax.vmap(lambda source: radial(source, target_where, atom_scale, filters))(
            source_where
        )
        atom_sums = jnp.einsum(
            "kcj,krji->rci", source_feat, kernel_rows, preferred_element_type=jnp.float32
        )
        atom_sums = atom_sums.astype(jnp.bfloat16).reshape(filters * channels, atom_width)
        message = jnp.dot(atom_filter, atom_sums, preferred_element_type=jnp.float32)
        updated = (
            (own_feat.astype(jnp.float32) + jax.nn.silu(message)) * own_mask[None, :]
        ).astype(jnp.bfloat16)
        return (updated, atom_sums, message)

    updated, atom_sums, message = lax.map(
        atom_block, (neighbour_rows, atom_pos, atom_feat, atom_mask)
    )
    stored_rows = jnp.concatenate([updated, atom_pos], axis=1)
    flat_owner = (tile_blocks // blocks_dev % tile_peers).reshape(-1)
    flat_spot = (tile_blocks % blocks_dev).reshape(-1)
    request_cap = max(2, 2 * reads_tile * tiles_dev // tile_peers)
    matches = (flat_owner[:, None, None] == jnp.arange(tile_peers)[None, :, None]) & (
        flat_spot[:, None, None] == jnp.arange(blocks_dev)[None, None, :]
    )
    needed_rows = jnp.any(matches, axis=0).astype(jnp.int32)
    rank_rows = jnp.cumsum(needed_rows, axis=1) - needed_rows
    chosen_rows = (needed_rows[:, None, :] == 1) & (
        rank_rows[:, None, :] == jnp.arange(request_cap)[None, :, None]
    )
    request_ids = jnp.sum(
        chosen_rows.astype(jnp.int32) * jnp.arange(blocks_dev)[None, None, :], axis=2
    )
    asked_ids = lax.all_to_all(request_ids, "tile", split_axis=0, concat_axis=0, tiled=True)
    sent_rows = jnp.take(stored_rows, asked_ids, axis=0)
    replies, asked_ids = (
        lax.all_to_all(sent_rows, "tile", split_axis=0, concat_axis=0, tiled=True),
        asked_ids,
    )
    slot_index = flat_owner * request_cap + rank_rows[flat_owner, flat_spot]
    slot_total = tile_peers * request_cap
    fetched = jnp.take(replies.reshape(slot_total, channels + 3, atom_width), slot_index, axis=0)
    fetched = fetched.reshape(tiles_dev, reads_tile, channels + 3, atom_width)
    probe_scale = (reads_tile * atom_width) ** (-0.5)

    def probe_tile(tile_index):
        tile_fetch = fetched[tile_index]
        probe_where = probe_pos[tile_index]
        source_where = tile_fetch[:, channels:].astype(jnp.float32)
        kernels = jax.vmap(lambda source: radial(source, probe_where, probe_scale, filters))(
            source_where
        )
        summed = jnp.einsum(
            "kca,krap->rcp", tile_fetch[:, :channels], kernels, preferred_element_type=jnp.float32
        )
        summed = summed.astype(jnp.bfloat16).reshape(filters * channels, probe_count)
        hidden = jnp.dot(probe_filter, summed, preferred_element_type=jnp.float32)
        squashed = jax.nn.silu(hidden).astype(jnp.bfloat16)
        mixed_rows = jnp.dot(mix_weight, squashed, preferred_element_type=jnp.float32)
        outer_act = jax.nn.silu(mixed_rows)
        density = jnp.dot(readout, outer_act, precision=highest)
        misfit = (density - probe_target[tile_index]) / probe_count
        grad_readout = jnp.dot(outer_act, misfit, precision=highest)
        grad_mixed = (readout[:, None] * misfit[None, :] * silu_slope(mixed_rows)).astype(
            jnp.bfloat16
        )
        grad_mix = jnp.dot(grad_mixed, squashed.T, preferred_element_type=jnp.float32)
        grad_squashed = jnp.dot(mix_weight.T, grad_mixed, preferred_element_type=jnp.float32)
        grad_hidden = (grad_squashed * silu_slope(hidden)).astype(jnp.bfloat16)
        grad_probe = jnp.dot(grad_hidden, summed.T, preferred_element_type=jnp.float32)
        grad_summed = jnp.dot(probe_filter.T, grad_hidden, preferred_element_type=jnp.float32)
        grad_summed = grad_summed.astype(jnp.bfloat16).reshape(filters, channels, probe_count)
        grad_blocks = jnp.einsum(
            "rcp,krap->kca", grad_summed, kernels, preferred_element_type=jnp.float32
        )
        return (density, grad_probe, grad_mix, grad_readout, grad_blocks)

    density, grad_probe, grad_mix, grad_readout, grad_blocks = lax.map(
        probe_tile, jnp.arange(tiles_dev)
    )
    grad_flat = grad_blocks.reshape(tiles_dev * reads_tile, channels, atom_width)
    pick_rows = (slot_index[None, :] == jnp.arange(slot_total)[:, None]).astype(jnp.float32)
    slot_grad = jnp.einsum("gs,sca->gca", pick_rows, grad_flat, precision=highest).astype(
        jnp.bfloat16
    )
    returned = lax.all_to_all(
        slot_grad.reshape(tile_peers, request_cap, channels, atom_width),
        "tile",
        split_axis=0,
        concat_axis=0,
        tiled=True,
    )
    owner_pick = (asked_ids[:, :, None] == jnp.arange(blocks_dev)[None, None, :]).astype(
        jnp.float32
    )
    block_grad = jnp.einsum(
        "tkb,tkca->bca", owner_pick, returned.astype(jnp.float32), precision=highest
    )
    grad_message = (block_grad * atom_mask[:, None, :] * silu_slope(message)).astype(jnp.bfloat16)
    grad_atom = jnp.einsum(
        "bca,bda->cd", grad_message, atom_sums, preferred_element_type=jnp.float32
    )
    totals = lax.psum(
        (
            grad_atom,
            jnp.sum(grad_probe, axis=0),
            jnp.sum(grad_mix, axis=0),
            jnp.sum(grad_readout, axis=0),
        ),
        ("space", "tile"),
    )
    return (density, totals[0], totals[1], totals[2], totals[3])


def solution(mesh):
    return jax.shard_map(
        body,
        mesh=mesh,
        in_specs=(
            P(("space", "tile"), None, None),
            P(("space", "tile"), None, None),
            P(("space", "tile")),
            P(("space", "tile"), None),
            P(("space", "tile"), None, None),
            P(("space", "tile"), None),
            P(("space", "tile"), None),
            P(),
            P(),
            P(),
            P(),
        ),
        out_specs=(P(("space", "tile"), None), P(), P(), P(), P()),
        check_vma=False,
    )
```

profile of v0, /device:TPU:0, one launch (start us, length us, event | category | flops | bytes accessed | tf_op | source)
XLA Modules:
  0.0 433.7 jit_solution(2652389257295615800)
XLA Ops:
  14.0 5.8 %all-to-all-start = ((s32[8,1,4]{2,1,0:T(1,128)}), s32[8,1,4]{2,1,0:T(1,128)S(1)}, u32[]{:S(2)}, u32[]{:S(2)}) async-start(s32[8,1,4]{2,1,0:T(1,128)} %copy.115), calls=%async_computation | async-start | bytes 8192 | tf_op jit(solution)/shard_map/all_to_all | solution.py:111
  20.2 6.0 %all-to-all-done = s32[8,1,4]{2,1,0:T(1,128)S(1)} async-done(((s32[8,1,4]{2,1,0:T(1,128)}), s32[8,1,4]{2,1,0:T(1,128)S(1)}, u32[]{:S(2)}, u32[]{:S(2)}) %all-to-all-start) | async-done | bytes 160 | tf_op jit(solution)/shard_map/all_to_all | solution.py:111
  31.6 114.4 %while.36 = (s32[]{:T(128)}, bf16[16,128,128]{2,1,0:T(8,128)(2,1)S(1)}, bf16[16,1024,128]{2,1,0:T(8,128)(2,1)}, f32[16,128,128]{2,0,1:T(8,128)}, bf16[16,128,128...) while((s32[]{:T(128)}, ...), condition=%wide.region_4.5_spmd, body=%wide.region_3.4_spmd.sunk | while | flops 172165008 | bytes 3516337 | solution.py:93
  35.8 2.9 dynamic_update_slice.71
  43.0 2.9 dynamic_update_slice.71
  50.1 2.9 dynamic_update_slice.71
  57.3 2.9 dynamic_update_slice.71
  64.4 2.9 dynamic_update_slice.71
  71.6 2.9 dynamic_update_slice.71
  78.8 2.9 dynamic_update_slice.71
  85.9 2.9 dynamic_update_slice.71
  93.1 2.9 dynamic_update_slice.71
  100.2 2.9 dynamic_update_slice.71
  107.4 2.9 dynamic_update_slice.71
  114.5 2.9 dynamic_update_slice.71
  121.7 2.9 dynamic_update_slice.71
  128.8 2.9 dynamic_update_slice.71
  135.9 2.9 dynamic_update_slice.71
  143.1 2.9 dynamic_update_slice.71
  149.0 5.3 %all-to-all-start.1 = ((bf16[8,4,131,128]{3,1,2,0:T(4,128)(2,1)}), bf16[8,4,131,128]{3,1,2,0:T(4,128)(2,1)S(1)}, u32[]{:S(2)}, u32[]{:S(2)}) async-start(bf16[8,4,131,128]{3,1,2,0:T(4,128)(2,1)} %copy.129), calls=%async_computation.1 | async-start | bytes 2146304 | tf_op jit(solution)/shard_map/all_to_all | solution.py:114
  155.8 24.4 %all-to-all-done.1 = bf16[8,4,131,128]{3,1,2,0:T(4,128)(2,1)S(1)} async-done(((bf16[8,4,131,128]{3,1,2,0:T(4,128)(2,1)}), bf16[8,4,131,128]{3,1,2,0:T(4,128)(2,1)S(1)}, u32[]{:S(2)}, u32[]{:S(2)}) %all-to-all-start.1) | async-done | bytes 1073184 | tf_op jit(solution)/shard_map/all_to_all | solution.py:114
  182.0 70.0 %while.37 = (s32[]{:T(128)}, f32[2,512]{1,0:T(2,128)S(1)}, f32[2,128,1024]{2,1,0:T(8,128)}, f32[2,128,128]{2,1,0:T(8,128)}, f32[2,128]{1,0:T(2,128)}, /*index=5*...) while((s32[]{:T(128)}, f32[2,512]{1,0:T(2,128)S(1)}, ...), condition=%wide.region_6.7_spmd, body=%wide.region_5.6_spmd.sunk | while | flops 2663714816 | bytes 38164880 | solution.py:155
  185.8 8.5 %add_sqrt_fusion.5 = (f32[8,128,512]{2,1,0:T(8,128)S(1)}, f32[8,128,512]{2,1,0:T(8,128)S(1)}) fusion(f32[512]{0:T(512)S(1)} %bitcast.288, f32[8,128]{1,0:T(8,128)S(1)} %bitcast.284, f32[512]{0:T(512)S(1)} %bitcast.287, f32[8,128]{1,0:T(8,128)S(1)} %bitcast.285, f32[512]{0:T(512)S(1)} %bitcast.286, f32[8,128]{1,0:T(8,128)S(1)} %bitcast.283), kind=kLoop, calls=%fused_computation.47.clone.2 | loop fusion | flops 7864320 | bytes 4212736 | tf_op jit(solution)/shard_map/while/body/eval_jaxpr/vmap()/sqrt | solution.py:35
  194.3 5.1 %bitcast_convert_fusion.2 = bf16[8,512,128]{1,2,0:T(8,128)(2,1)S(1)} fusion(f32[8,128,512]{2,1,0:T(8,128)S(1)} %get-tuple-element.580, f32[8]{0:T(128)S(1)} %convert_multiply_fusion.5, f32[8,128,512]{2,1,0:T(8,128)S(1)} %get-tuple-element.581, bf16[8,131,128]{2,1,0:T(8,128)(2,1)S(1)} %dynamic-slice_bitcast_fusion.5), kind=kOutput, calls=%fused_computation.45.clone.1 | convolution fusion | flops 1099431936 | bytes 5505536 | tf_op jit(solution)/shard_map/while/body/eval_jaxpr/kca,krap->rcp/dot_general | solution.py:130
  210.0 7.0 %fusion.163 = f32[2,8,128,128]{2,3,1,0:T(8,128)} fusion(f32[2,8,128,128]{2,3,1,0:T(8,128)} %get-tuple-element.638, s32[]{:T(128)S(6)} %copy.188, bf16[8,128,512,1]{2,1,0,3:T(8,128)(2,1)} %bitcast.273, f32[8,128,512]{2,1,0:T(8,128)} %copy-done, f32[8]{0:T(128)} %copy-done.31, f32[8,128,512]{2,1,0:T(8,128)S(1)} %get-tuple-element.581), kind=kOutput, calls=%fused_computation.51.clone.1 | convolution fusion | flops 1098907648 | bytes 5767684 | tf_op jit(solution)/shard_map/while/body/eval_jaxpr/rcp,krap->kca/dot_general | solution.py:150
  220.6 8.5 %add_sqrt_fusion.5 = (f32[8,128,512]{2,1,0:T(8,128)S(1)}, f32[8,128,512]{2,1,0:T(8,128)S(1)}) fusion(f32[512]{0:T(512)S(1)} %bitcast.288, f32[8,128]{1,0:T(8,128)S(1)} %bitcast.284, f32[512]{0:T(512)S(1)} %bitcast.287, f32[8,128]{1,0:T(8,128)S(1)} %bitcast.285, f32[512]{0:T(512)S(1)} %bitcast.286, f32[8,128]{1,0:T(8,128)S(1)} %bitcast.283), kind=kLoop, calls=%fused_computation.47.clone.2 | loop fusion | flops 7864320 | bytes 4212736 | tf_op jit(solution)/shard_map/while/body/eval_jaxpr/vmap()/sqrt | solution.py:35
  229.1 5.1 %bitcast_convert_fusion.2 = bf16[8,512,128]{1,2,0:T(8,128)(2,1)S(1)} fusion(f32[8,128,512]{2,1,0:T(8,128)S(1)} %get-tuple-element.580, f32[8]{0:T(128)S(1)} %convert_multiply_fusion.5, f32[8,128,512]{2,1,0:T(8,128)S(1)} %get-tuple-element.581, bf16[8,131,128]{2,1,0:T(8,128)(2,1)S(1)} %dynamic-slice_bitcast_fusion.5), kind=kOutput, calls=%fused_computation.45.clone.1 | convolution fusion | flops 1099431936 | bytes 5505536 | tf_op jit(solution)/shard_map/while/body/eval_jaxpr/kca,krap->rcp/dot_general | solution.py:130
  244.8 7.0 %fusion.163 = f32[2,8,128,128]{2,3,1,0:T(8,128)} fusion(f32[2,8,128,128]{2,3,1,0:T(8,128)} %get-tuple-element.638, s32[]{:T(128)S(6)} %copy.188, bf16[8,128,512,1]{2,1,0,3:T(8,128)(2,1)} %bitcast.273, f32[8,128,512]{2,1,0:T(8,128)} %copy-done, f32[8]{0:T(128)} %copy-done.31, f32[8,128,512]{2,1,0:T(8,128)S(1)} %get-tuple-element.581), kind=kOutput, calls=%fused_computation.51.clone.1 | convolution fusion | flops 1098907648 | bytes 5767684 | tf_op jit(solution)/shard_map/while/body/eval_jaxpr/rcp,krap->kca/dot_general | solution.py:150
  256.4 3.7 all-to-all-start.2
  261.8 24.1 %all-to-all-done.2 = bf16[8,4,128,128]{3,1,2,0:T(4,128)(2,1)S(1)} async-done(((bf16[8,4,128,128]{3,1,2,0:T(4,128)(2,1)}), bf16[8,4,128,128]{3,1,2,0:T(4,128)(2,1)S(1)}, u32[]{:S(2)}, u32[]{:S(2)}) %all-to-all-start.2) | async-done | bytes 1048608 | tf_op jit(solution)/shard_map/all_to_all | solution.py:163
  290.4 38.8 %psum.31 = f32[128]{0:T(128)} all-reduce(f32[128]{0:T(128)S(1)} %reduce_sum.39), channel_id=1, replica_groups=mesh['space'=4,'tile'=8] {'space','tile'}, use_global_device_ids=true, to_apply=%region_13.14 | all-reduce | flops 128 | bytes 1024 | tf_op jit(solution)/shard_map/psum | solution.py:180
  329.2 93.2 %all-reduce.3.cloned.1.call-done = (f32[128,1024]{1,0:T(8,128)}, f32[128,1024]{1,0:T(8,128)}, f32[128,128]{1,0:T(8,128)}) async-done(((f32[128,1024]{1,0:T(8,128)}, f32[128,1024]{1,0:T(8,128)}, f32[128,128]{1,0:T(8,128)}), (f32[128,1024]{1,0:T(8,128)}, f32[128,1024]{1,0:T(8,128)}, f32[128,128]{1,0:T(8,128)})) %all-reduce.3.cloned.1.call-update) | async-done | bytes 1114128 | tf_op jit(solution)/shard_map/psum | solution.py:180
  (480 shorter events, 123.5 us)
Async XLA Ops:
  7.2 12.7 %copy-start.10 = (bf16[16,3,128]{2,0,1:T(8,128)(2,1)S(1)}, bf16[16,3,128]{2,0,1:T(8,128)(2,1)}, u32[]{:S(2)}) copy-start(bf16[16,3,128]{2,0,1:T(8,128)(2,1)} %param.16) | copy-start | bytes 36868
  7.2 5.4 %copy-start.18 = (s32[2,8]{1,0:T(2,128)S(1)}, s32[2,8]{1,0:T(2,128)}, u32[]{:S(2)}) copy-start(s32[2,8]{1,0:T(2,128)} %param.21) | copy-start | bytes 196
  7.2 12.7 %copy-start.17 = (s32[16,4]{0,1:T(4,128)S(1)}, s32[16,4]{0,1:T(4,128)}, u32[]{:S(2)}) copy-start(s32[16,4]{0,1:T(4,128)} %param.18) | copy-start | bytes 772
  10.1 16.5 %collective-permute-start.1 = (bf16[16,131,128]{2,0,1:T(8,128)(2,1)S(1)}, bf16[16,131,128]{2,0,1:T(8,128)(2,1)S(1)}, u32[]{:S(2)}, u32[]{:S(2)}) collective-permute-start(bf16[16,131,128]{2,0,1:T(8,128)(2,1)S(1)} %pad_maximum_fusion.2), channel_id=1, source_target_pairs={{8,0},{16,8},{24,16},{0,24},{9,1},{17,9},{25,17},{1,25},{10,2},{18... | collective-permute-start | bytes 1609736 | tf_op jit(solution)/shard_map/ppermute | solution.py:20
  12.5 14.1 %collective-permute-start = (bf16[16,131,128]{2,0,1:T(8,128)(2,1)S(1)}, bf16[16,131,128]{2,0,1:T(8,128)(2,1)S(1)}, u32[]{:S(2)}, u32[]{:S(2)}) collective-permute-start(bf16[16,131,128]{2,0,1:T(8,128)(2,1)S(1)} %pad_maximum_fusion.2), channel_id=1, source_target_pairs={{0,8},{8,16},{16,24},{24,0},{1,9},{9,17},{17,25},{25,1},{2,10},{10... | collective-permute-start | bytes 1609736 | tf_op jit(solution)/shard_map/ppermute | solution.py:17
  14.0 12.3 %all-to-all-start = ((s32[8,1,4]{2,1,0:T(1,128)}), s32[8,1,4]{2,1,0:T(1,128)S(1)}, u32[]{:S(2)}, u32[]{:S(2)}) async-start(s32[8,1,4]{2,1,0:T(1,128)} %copy.115), calls=%async_computation | async-start | bytes 8192 | tf_op jit(solution)/shard_map/all_to_all | solution.py:111
  149.0 31.2 %all-to-all-start.1 = ((bf16[8,4,131,128]{3,1,2,0:T(4,128)(2,1)}), bf16[8,4,131,128]{3,1,2,0:T(4,128)(2,1)S(1)}, u32[]{:S(2)}, u32[]{:S(2)}) async-start(bf16[8,4,131,128]{3,1,2,0:T(4,128)(2,1)} %copy.129), calls=%async_computation.1 | async-start | bytes 2146304 | tf_op jit(solution)/shard_map/all_to_all | solution.py:114
  155.8 26.2 %copy-start.1 = (bf16[128,1024]{1,0:T(8,128)(2,1)S(1)}, bf16[128,1024]{1,0:T(8,128)(2,1)}, u32[]{:S(2)}) copy-start(bf16[128,1024]{1,0:T(8,128)(2,1)} %param.23) | copy-start | bytes 786436
  155.8 26.2 %copy-start.11 = (f32[2,3,512]{2,0,1:T(2,128)S(1)}, f32[2,3,512]{2,0,1:T(2,128)}, u32[]{:S(2)}) copy-start(f32[2,3,512]{2,0,1:T(2,128)} %param.19) | copy-start | bytes 36868
  155.8 26.2 %copy-start.15 = (f32[128]{0:T(128)S(1)}, f32[128]{0:T(128)}, u32[]{:S(2)}) copy-start(f32[128]{0:T(128)} %param.25) | copy-start | bytes 1540
  155.8 26.2 %copy-start.24 = (bf16[128,128]{1,0:T(8,128)(2,1)S(1)}, bf16[128,128]{1,0:T(8,128)(2,1)}, u32[]{:S(2)}) copy-start(bf16[128,128]{1,0:T(8,128)(2,1)} %param.24) | copy-start | bytes 98308
  182.2 12.1 %copy-start.29 = (s32[2]{0:T(128)}, s32[2]{0:T(128)S(1)}, u32[]{:S(2)}) copy-start(s32[2]{0:T(128)S(1)} %get-tuple-element.657) | copy-start | bytes 28 | tf_op jit(solution)/shard_map/while
  194.3 5.2 %copy-start = (f32[8,128,512]{2,1,0:T(8,128)}, f32[8,128,512]{2,1,0:T(8,128)S(1)}, u32[]{:S(2)}) copy-start(f32[8,128,512]{2,1,0:T(8,128)S(1)} %get-tuple-element.580) | copy-start | bytes 6291460 | tf_op jit(solution)/shard_map/while
  194.3 5.2 %copy-start.31 = (f32[8]{0:T(128)}, f32[8]{0:T(128)S(1)}, u32[]{:S(2)}) copy-start(f32[8]{0:T(128)S(1)} %convert_multiply_fusion.5) | copy-start | bytes 100 | tf_op jit(solution)/shard_map/while
  202.0 4.4 %copy-start.6 = (f32[128,512]{0,1:T(8,128)S(1)}, f32[128,512]{0,1:T(8,128)}, u32[]{:S(2)}) copy-start(f32[128,512]{0,1:T(8,128)} %copy-done.5) | copy-start | bytes 786436 | tf_op jit(solution)/shard_map/while
  210.0 7.0 %copy-start.16 = (f32[128]{0:T(128)S(1)}, f32[128]{0:T(128)}, u32[]{:S(2)}) copy-start(f32[128]{0:T(128)} %get-tuple-element.715) | copy-start | bytes 1540 | tf_op jit(solution)/shard_map/while
  210.0 7.0 %copy-start.25 = (bf16[128,128]{1,0:T(8,128)(2,1)S(1)}, bf16[128,128]{1,0:T(8,128)(2,1)}, u32[]{:S(2)}) copy-start(bf16[128,128]{1,0:T(8,128)(2,1)} %get-tuple-element.735) | copy-start | bytes 98308 | tf_op jit(solution)/shard_map/while
  210.0 7.0 %copy-start.27 = (f32[2,512]{1,0:T(2,128)S(1)}, f32[2,512]{1,0:T(2,128)}, u32[]{:S(2)}) copy-start(f32[2,512]{1,0:T(2,128)} %copy-done.26) | copy-start | bytes 12292 | tf_op jit(solution)/shard_map/while
  210.0 7.0 %copy-start.30 = (s32[2]{0:T(128)S(1)}, s32[2]{0:T(128)}, u32[]{:S(2)}) copy-start(s32[2]{0:T(128)} %copy-done.29) | copy-start | bytes 28 | tf_op jit(solution)/shard_map/while
  217.0 12.1 %copy-start.29 = (s32[2]{0:T(128)}, s32[2]{0:T(128)S(1)}, u32[]{:S(2)}) copy-start(s32[2]{0:T(128)S(1)} %get-tuple-element.657) | copy-start | bytes 28 | tf_op jit(solution)/shard_map/while
  229.1 5.2 %copy-start = (f32[8,128,512]{2,1,0:T(8,128)}, f32[8,128,512]{2,1,0:T(8,128)S(1)}, u32[]{:S(2)}) copy-start(f32[8,128,512]{2,1,0:T(8,128)S(1)} %get-tuple-element.580) | copy-start | bytes 6291460 | tf_op jit(solution)/shard_map/while
  229.1 5.2 %copy-start.31 = (f32[8]{0:T(128)}, f32[8]{0:T(128)S(1)}, u32[]{:S(2)}) copy-start(f32[8]{0:T(128)S(1)} %convert_multiply_fusion.5) | copy-start | bytes 100 | tf_op jit(solution)/shard_map/while
  244.8 7.0 %copy-start.16 = (f32[128]{0:T(128)S(1)}, f32[128]{0:T(128)}, u32[]{:S(2)}) copy-start(f32[128]{0:T(128)} %get-tuple-element.715) | copy-start | bytes 1540 | tf_op jit(solution)/shard_map/while
  244.8 7.0 %copy-start.25 = (bf16[128,128]{1,0:T(8,128)(2,1)S(1)}, bf16[128,128]{1,0:T(8,128)(2,1)}, u32[]{:S(2)}) copy-start(bf16[128,128]{1,0:T(8,128)(2,1)} %get-tuple-element.735) | copy-start | bytes 98308 | tf_op jit(solution)/shard_map/while
  244.8 7.0 %copy-start.27 = (f32[2,512]{1,0:T(2,128)S(1)}, f32[2,512]{1,0:T(2,128)}, u32[]{:S(2)}) copy-start(f32[2,512]{1,0:T(2,128)} %copy-done.26) | copy-start | bytes 12292 | tf_op jit(solution)/shard_map/while
  244.8 7.0 %copy-start.30 = (s32[2]{0:T(128)S(1)}, s32[2]{0:T(128)}, u32[]{:S(2)}) copy-start(s32[2]{0:T(128)} %copy-done.29) | copy-start | bytes 28 | tf_op jit(solution)/shard_map/while
  254.9 5.3 %copy-start.8 = (f32[2,128,1024]{2,1,0:T(8,128)S(1)}, f32[2,128,1024]{2,1,0:T(8,128)}, u32[]{:S(2)}) copy-start(f32[2,128,1024]{2,1,0:T(8,128)} %get-tuple-element.718) | copy-start | bytes 3145732
  256.4 4.7 %copy-start.9 = (f32[2,128,128]{2,1,0:T(8,128)S(1)}, f32[2,128,128]{2,1,0:T(8,128)}, u32[]{:S(2)}) copy-start(f32[2,128,128]{2,1,0:T(8,128)} %get-tuple-element.719) | copy-start | bytes 393220
  256.4 29.5 %copy-start.14 = (f32[16,128]{1,0:T(8,128)S(1)}, f32[16,128]{1,0:T(8,128)}, u32[]{:S(2)}) copy-start(f32[16,128]{1,0:T(8,128)} %copy-done.13) | copy-start | bytes 24580
  256.4 29.5 %copy-start.23 = (f32[16,128,128]{2,0,1:T(8,128)S(1)}, f32[16,128,128]{2,0,1:T(8,128)}, u32[]{:S(2)}) copy-start(f32[16,128,128]{2,0,1:T(8,128)} %get-tuple-element.288) | copy-start | bytes 3145732
  256.4 29.5 %all-to-all-start.2 = ((bf16[8,4,128,128]{3,1,2,0:T(4,128)(2,1)}), bf16[8,4,128,128]{3,1,2,0:T(4,128)(2,1)S(1)}, u32[]{:S(2)}, u32[]{:S(2)}) async-start(bf16[8,4,128,128]{3,1,2,0:T(4,128)(2,1)} %copy.133), calls=%async_computation.2 | async-start | bytes 2097152 | tf_op jit(solution)/shard_map/all_to_all | solution.py:163
  260.1 162.3 %all-reduce.3.cloned.1.call-start = ((), (), s32[]{:S(2)}) async-start(), calls=%async_computation.3 | async-start | bytes 2228224 | tf_op jit(solution)/shard_map/psum | solution.py:180
  (20 other events, 34.9 us)
Sparse Core Ops, SparseCore 0:
  290.5 131.8 all-reduce.2
where the time goes:
time: 436 us; the launch traced here: 434 us
  waiting for transfers between devices  148 us (34%)
  local copies, waits for them, and re-layouts  105 us (24%)
  matrix products  55.9 us (13%)
  other arithmetic  47.9 us (11%)
  blocking collectives  38.8 us (9%)
  starting transfers between devices  17.4 us (4%)
  between operations  14.4 us (3%)
  loops' own time  6.15 us (1%)
    psum x1, waiting for transfers between devices, body(): lax.psum((grad_atom, jnp.sum(grad_probe, axis=0), jnp.sum(grad_mix, axis=...  93.2 us
    dynamic_update_slice x80, local copies, waits for them, and re-layouts, body(): lax.map(atom_block, (neighbour_rows, atom_pos, atom_feat, atom_mask))  62.2 us
    psum x1, blocking collectives, body(): lax.psum((grad_atom, jnp.sum(grad_probe, axis=0), jnp.sum(grad_mix, axis=...  38.8 us
    sqrt x18, other arithmetic, radial(): distance = jnp.sqrt(square + 0.01)  34.7 us
    all_to_all x1, waiting for transfers between devices, body(): lax.all_to_all(sent_rows, 'tile', split_axis=0, concat_axis=0, tiled=True)  24.4 us
    all_to_all x1, waiting for transfers between devices, body(): lax.all_to_all(slot_grad.reshape(tile_peers, request_cap, channels, atom_...  24.1 us
    dynamic_slice x32, local copies, waits for them, and re-layouts, body(): lax.map(atom_block, (neighbour_rows, atom_pos, atom_feat, atom_mask))  14 us
    dot_general x2, matrix products, probe_tile(): jnp.einsum('rcp,krap->kca', grad_summed, kernels, preferred_element_type=...  14 us
  transfers between devices with their start and end apart: 6, of which 4 were waited for; matrix products, arithmetic and copies ran while one was open for 1% of the time, Pallas kernels for 0%

commit v1 on v0

--- a/solution.py
+++ b/solution.py
@@ -177,15 +177,16 @@
     grad_atom = jnp.einsum(
         "bca,bda->cd", grad_message, atom_sums, preferred_element_type=jnp.float32
     )
-    totals = lax.psum(
+    inner = lax.psum(
         (
             grad_atom,
             jnp.sum(grad_probe, axis=0),
             jnp.sum(grad_mix, axis=0),
             jnp.sum(grad_readout, axis=0),
         ),
-        ("space", "tile"),
-    )
+        "tile",
+    )
+    totals = lax.psum(inner, "space")
     return (density, totals[0], totals[1], totals[2], totals[3])
 
 

time: 436 us -> 422 us (0.968)
  blocking collectives: 38.8 us -> 26.1 us
    psum x1, blocking collectives: 38.8 us -> 19.9 us  [body(): lax.psum((grad_atom, jnp.sum(grad_probe, axis=0), jnp.sum(grad_mix, axis=...]
    psum x1, waiting for transfers between devices: 93.2 us -> 79.4 us  [body(): lax.psum((grad_atom, jnp.sum(grad_probe, axis=0), jnp.sum(grad_mix, axis=...]
    psum x0 -> x1, waiting for transfers between devices: none -> 12.9 us  [body(): totals = lax.psum(inner, 'space')]
    psum x0 -> x1, blocking collectives: none -> 6.15 us  [body(): totals = lax.psum(inner, 'space')]
  transfers between devices with their start and end apart: 6 -> 7, of which waited for: 4 -> 5; matrix products, arithmetic and copies ran while one was open for 1% -> 1% of each run, Pallas kernels for 0% -> 0%
where the time goes in v1:
time: 422 us; the launch traced here: 420 us
  waiting for transfers between devices  147 us (35%)
  local copies, waits for them, and re-layouts  105 us (25%)
  matrix products  55.9 us (13%)
  other arithmetic  47.9 us (11%)
  blocking collectives  26.1 us (6%)
  starting transfers between devices  17.4 us (4%)
  between operations  14.4 us (3%)
  loops' own time  6.16 us (1%)
    psum x1, waiting for transfers between devices, body(): lax.psum((grad_atom, jnp.sum(grad_probe, axis=0), jnp.sum(grad_mix, axis=...  79.4 us
    dynamic_update_slice x80, local copies, waits for them, and re-layouts, body(): lax.map(atom_block, (neighbour_rows, atom_pos, atom_feat, atom_mask))  62.1 us
    sqrt x18, other arithmetic, radial(): distance = jnp.sqrt(square + 0.01)  34.7 us
    all_to_all x1, waiting for transfers between devices, body(): lax.all_to_all(sent_rows, 'tile', split_axis=0, concat_axis=0, tiled=True)  24.4 us
    all_to_all x1, waiting for transfers between devices, body(): lax.all_to_all(slot_grad.reshape(tile_peers, request_cap, channels, atom_...  24.1 us
    psum x1, blocking collectives, body(): lax.psum((grad_atom, jnp.sum(grad_probe, axis=0), jnp.sum(grad_mix, axis=...  19.9 us
    dynamic_slice x32, local copies, waits for them, and re-layouts, body(): lax.map(atom_block, (neighbour_rows, atom_pos, atom_feat, atom_mask))  14 us
    dot_general x2, matrix products, probe_tile(): jnp.einsum('rcp,krap->kca', grad_summed, kernels, preferred_element_type=...  13.9 us
  transfers between devices with their start and end apart: 7, of which 5 were waited for; matrix products, arithmetic and copies ran while one was open for 1% of the time, Pallas kernels for 0%

profile of v1, /device:TPU:0, one launch (start us, length us, event | category | flops | bytes accessed | tf_op | source)
XLA Modules:
  0.0 420.0 jit_solution(3685510557698415716)
XLA Ops:
  14.0 5.8 %all-to-all-start = ((s32[8,1,4]{2,1,0:T(1,128)}), s32[8,1,4]{2,1,0:T(1,128)S(1)}, u32[]{:S(2)}, u32[]{:S(2)}) async-start(s32[8,1,4]{2,1,0:T(1,128)} %copy.115), calls=%async_computation | async-start | bytes 8192 | tf_op jit(solution)/shard_map/all_to_all | solution.py:111
  20.2 6.0 %all-to-all-done = s32[8,1,4]{2,1,0:T(1,128)S(1)} async-done(((s32[8,1,4]{2,1,0:T(1,128)}), s32[8,1,4]{2,1,0:T(1,128)S(1)}, u32[]{:S(2)}, u32[]{:S(2)}) %all-to-all-start) | async-done | bytes 160 | tf_op jit(solution)/shard_map/all_to_all | solution.py:111
  31.6 114.4 %while.36 = (s32[]{:T(128)}, bf16[16,128,128]{2,1,0:T(8,128)(2,1)S(1)}, bf16[16,1024,128]{2,1,0:T(8,128)(2,1)}, f32[16,128,128]{2,0,1:T(8,128)}, bf16[16,128,128...) while((s32[]{:T(128)}, ...), condition=%wide.region_4.5_spmd, body=%wide.region_3.4_spmd.sunk | while | flops 172165008 | bytes 3516337 | solution.py:93
  35.8 2.9 dynamic_update_slice.71
  43.0 2.9 dynamic_update_slice.71
  50.2 2.9 dynamic_update_slice.71
  57.3 2.9 dynamic_update_slice.71
  64.5 2.9 dynamic_update_slice.71
  71.6 2.9 dynamic_update_slice.71
  78.8 2.9 dynamic_update_slice.71
  85.9 2.9 dynamic_update_slice.71
  93.1 2.9 dynamic_update_slice.71
  100.2 2.9 dynamic_update_slice.71
  107.4 2.9 dynamic_update_slice.71
  114.5 2.9 dynamic_update_slice.71
  121.7 2.9 dynamic_update_slice.71
  135.9 2.9 dynamic_update_slice.71
  148.9 5.3 %all-to-all-start.1 = ((bf16[8,4,131,128]{3,1,2,0:T(4,128)(2,1)}), bf16[8,4,131,128]{3,1,2,0:T(4,128)(2,1)S(1)}, u32[]{:S(2)}, u32[]{:S(2)}) async-start(bf16[8,4,131,128]{3,1,2,0:T(4,128)(2,1)} %copy.129), calls=%async_computation.1 | async-start | bytes 2146304 | tf_op jit(solution)/shard_map/all_to_all | solution.py:114
  155.7 24.4 %all-to-all-done.1 = bf16[8,4,131,128]{3,1,2,0:T(4,128)(2,1)S(1)} async-done(((bf16[8,4,131,128]{3,1,2,0:T(4,128)(2,1)}), bf16[8,4,131,128]{3,1,2,0:T(4,128)(2,1)S(1)}, u32[]{:S(2)}, u32[]{:S(2)}) %all-to-all-start.1) | async-done | bytes 1073184 | tf_op jit(solution)/shard_map/all_to_all | solution.py:114
  181.9 70.0 %while.37 = (s32[]{:T(128)}, f32[2,512]{1,0:T(2,128)S(1)}, f32[2,128,1024]{2,1,0:T(8,128)}, f32[2,128,128]{2,1,0:T(8,128)}, f32[2,128]{1,0:T(2,128)}, /*index=5*...) while((s32[]{:T(128)}, f32[2,512]{1,0:T(2,128)S(1)}, ...), condition=%wide.region_6.7_spmd, body=%wide.region_5.6_spmd.sunk | while | flops 2663714816 | bytes 38164880 | solution.py:155
  185.7 8.5 %add_sqrt_fusion.5 = (f32[8,128,512]{2,1,0:T(8,128)S(1)}, f32[8,128,512]{2,1,0:T(8,128)S(1)}) fusion(f32[512]{0:T(512)S(1)} %bitcast.288, f32[8,128]{1,0:T(8,128)S(1)} %bitcast.284, f32[512]{0:T(512)S(1)} %bitcast.287, f32[8,128]{1,0:T(8,128)S(1)} %bitcast.285, f32[512]{0:T(512)S(1)} %bitcast.286, f32[8,128]{1,0:T(8,128)S(1)} %bitcast.283), kind=kLoop, calls=%fused_computation.47.clone.2 | loop fusion | flops 7864320 | bytes 4212736 | tf_op jit(solution)/shard_map/while/body/eval_jaxpr/vmap()/sqrt | solution.py:35
  194.2 5.1 %bitcast_convert_fusion.2 = bf16[8,512,128]{1,2,0:T(8,128)(2,1)S(1)} fusion(f32[8,128,512]{2,1,0:T(8,128)S(1)} %get-tuple-element.583, f32[8]{0:T(128)S(1)} %convert_multiply_fusion.5, f32[8,128,512]{2,1,0:T(8,128)S(1)} %get-tuple-element.584, bf16[8,131,128]{2,1,0:T(8,128)(2,1)S(1)} %dynamic-slice_bitcast_fusion.5), kind=kOutput, calls=%fused_computation.45.clone.1 | convolution fusion | flops 1099431936 | bytes 5505536 | tf_op jit(solution)/shard_map/while/body/eval_jaxpr/kca,krap->rcp/dot_general | solution.py:130
  209.9 7.0 %fusion.163 = f32[2,8,128,128]{2,3,1,0:T(8,128)} fusion(f32[2,8,128,128]{2,3,1,0:T(8,128)} %get-tuple-element.641, s32[]{:T(128)S(6)} %copy.188, bf16[8,128,512,1]{2,1,0,3:T(8,128)(2,1)} %bitcast.273, f32[8,128,512]{2,1,0:T(8,128)} %copy-done, f32[8]{0:T(128)} %copy-done.31, f32[8,128,512]{2,1,0:T(8,128)S(1)} %get-tuple-element.584), kind=kOutput, calls=%fused_computation.51.clone.1 | convolution fusion | flops 1098907648 | bytes 5767684 | tf_op jit(solution)/shard_map/while/body/eval_jaxpr/rcp,krap->kca/dot_general | solution.py:150
  220.5 8.5 %add_sqrt_fusion.5 = (f32[8,128,512]{2,1,0:T(8,128)S(1)}, f32[8,128,512]{2,1,0:T(8,128)S(1)}) fusion(f32[512]{0:T(512)S(1)} %bitcast.288, f32[8,128]{1,0:T(8,128)S(1)} %bitcast.284, f32[512]{0:T(512)S(1)} %bitcast.287, f32[8,128]{1,0:T(8,128)S(1)} %bitcast.285, f32[512]{0:T(512)S(1)} %bitcast.286, f32[8,128]{1,0:T(8,128)S(1)} %bitcast.283), kind=kLoop, calls=%fused_computation.47.clone.2 | loop fusion | flops 7864320 | bytes 4212736 | tf_op jit(solution)/shard_map/while/body/eval_jaxpr/vmap()/sqrt | solution.py:35
  229.0 5.1 %bitcast_convert_fusion.2 = bf16[8,512,128]{1,2,0:T(8,128)(2,1)S(1)} fusion(f32[8,128,512]{2,1,0:T(8,128)S(1)} %get-tuple-element.583, f32[8]{0:T(128)S(1)} %convert_multiply_fusion.5, f32[8,128,512]{2,1,0:T(8,128)S(1)} %get-tuple-element.584, bf16[8,131,128]{2,1,0:T(8,128)(2,1)S(1)} %dynamic-slice_bitcast_fusion.5), kind=kOutput, calls=%fused_computation.45.clone.1 | convolution fusion | flops 1099431936 | bytes 5505536 | tf_op jit(solution)/shard_map/while/body/eval_jaxpr/kca,krap->rcp/dot_general | solution.py:130
  244.7 7.0 %fusion.163 = f32[2,8,128,128]{2,3,1,0:T(8,128)} fusion(f32[2,8,128,128]{2,3,1,0:T(8,128)} %get-tuple-element.641, s32[]{:T(128)S(6)} %copy.188, bf16[8,128,512,1]{2,1,0,3:T(8,128)(2,1)} %bitcast.273, f32[8,128,512]{2,1,0:T(8,128)} %copy-done, f32[8]{0:T(128)} %copy-done.31, f32[8,128,512]{2,1,0:T(8,128)S(1)} %get-tuple-element.584), kind=kOutput, calls=%fused_computation.51.clone.1 | convolution fusion | flops 1098907648 | bytes 5767684 | tf_op jit(solution)/shard_map/while/body/eval_jaxpr/rcp,krap->kca/dot_general | solution.py:150
  256.3 3.7 all-to-all-start.2
  261.7 24.1 %all-to-all-done.2 = bf16[8,4,128,128]{3,1,2,0:T(4,128)(2,1)S(1)} async-done(((bf16[8,4,128,128]{3,1,2,0:T(4,128)(2,1)}), bf16[8,4,128,128]{3,1,2,0:T(4,128)(2,1)S(1)}, u32[]{:S(2)}, u32[]{:S(2)}) %all-to-all-start.2) | async-done | bytes 1048608 | tf_op jit(solution)/shard_map/all_to_all | solution.py:163
  290.3 79.4 %all-reduce.5.cloned.1.call-done = (f32[128,1024]{1,0:T(8,128)}, f32[128,1024]{1,0:T(8,128)}, f32[128,128]{1,0:T(8,128)}) async-done(((f32[128,1024]{1,0:T(8,128)}, f32[128,1024]{1,0:T(8,128)}, f32[128,128]{1,0:T(8,128)}), (f32[128,1024]{1,0:T(8,128)}, f32[128,1024]{1,0:T(8,128)}, f32[128,128]{1,0:T(8,128)})) %all-reduce.5.cloned.1.call-update) | async-done | bytes 1114128 | tf_op jit(solution)/shard_map/psum | solution.py:180
  369.7 19.9 %psum.62 = f32[128]{0:T(128)S(1)} all-reduce(f32[128]{0:T(128)S(1)} %reduce_sum.39), channel_id=1, replica_groups=mesh['space'=4,'tile'=8] {'tile'}, use_global_device_ids=true, to_apply=%region_16.17 | all-reduce | flops 128 | bytes 1024 | tf_op jit(solution)/shard_map/psum | solution.py:180
  389.7 6.2 %psum.63 = f32[128]{0:T(128)} all-reduce(f32[128]{0:T(128)S(1)} %psum.62), channel_id=1, replica_groups=mesh['space'=4,'tile'=8] {'space'}, use_global_device_ids=true, to_apply=%region_17.18 | all-reduce | flops 128 | bytes 1024 | tf_op jit(solution)/shard_map/psum | solution.py:189
  395.8 12.9 %all-reduce.7.cloned.1.call-done = (f32[128,1024]{1,0:T(8,128)}, f32[128,1024]{1,0:T(8,128)}, f32[128,128]{1,0:T(8,128)}) async-done(((f32[128,1024]{1,0:T(8,128)}, f32[128,1024]{1,0:T(8,128)}, f32[128,128]{1,0:T(8,128)}), (f32[128,1024]{1,0:T(8,128)}, f32[128,1024]{1,0:T(8,128)}, f32[128,128]{1,0:T(8,128)})) %all-reduce.7.cloned.1.call-update) | async-done | bytes 1114128 | tf_op jit(solution)/shard_map/psum | solution.py:189
  (484 shorter events, 129.3 us)
Async XLA Ops:
  7.2 12.7 %copy-start.10 = (bf16[16,3,128]{2,0,1:T(8,128)(2,1)S(1)}, bf16[16,3,128]{2,0,1:T(8,128)(2,1)}, u32[]{:S(2)}) copy-start(bf16[16,3,128]{2,0,1:T(8,128)(2,1)} %param.16) | copy-start | bytes 36868
  7.2 5.4 %copy-start.18 = (s32[2,8]{1,0:T(2,128)S(1)}, s32[2,8]{1,0:T(2,128)}, u32[]{:S(2)}) copy-start(s32[2,8]{1,0:T(2,128)} %param.21) | copy-start | bytes 196
  7.2 12.7 %copy-start.17 = (s32[16,4]{0,1:T(4,128)S(1)}, s32[16,4]{0,1:T(4,128)}, u32[]{:S(2)}) copy-start(s32[16,4]{0,1:T(4,128)} %param.18) | copy-start | bytes 772
  10.1 16.5 %collective-permute-start.1 = (bf16[16,131,128]{2,0,1:T(8,128)(2,1)S(1)}, bf16[16,131,128]{2,0,1:T(8,128)(2,1)S(1)}, u32[]{:S(2)}, u32[]{:S(2)}) collective-permute-start(bf16[16,131,128]{2,0,1:T(8,128)(2,1)S(1)} %pad_maximum_fusion.2), channel_id=1, source_target_pairs={{8,0},{16,8},{24,16},{0,24},{9,1},{17,9},{25,17},{1,25},{10,2},{18... | collective-permute-start | bytes 1609736 | tf_op jit(solution)/shard_map/ppermute | solution.py:20
  12.5 14.1 %collective-permute-start = (bf16[16,131,128]{2,0,1:T(8,128)(2,1)S(1)}, bf16[16,131,128]{2,0,1:T(8,128)(2,1)S(1)}, u32[]{:S(2)}, u32[]{:S(2)}) collective-permute-start(bf16[16,131,128]{2,0,1:T(8,128)(2,1)S(1)} %pad_maximum_fusion.2), channel_id=1, source_target_pairs={{0,8},{8,16},{16,24},{24,0},{1,9},{9,17},{17,25},{25,1},{2,10},{10... | collective-permute-start | bytes 1609736 | tf_op jit(solution)/shard_map/ppermute | solution.py:17
  14.0 12.3 %all-to-all-start = ((s32[8,1,4]{2,1,0:T(1,128)}), s32[8,1,4]{2,1,0:T(1,128)S(1)}, u32[]{:S(2)}, u32[]{:S(2)}) async-start(s32[8,1,4]{2,1,0:T(1,128)} %copy.115), calls=%async_computation | async-start | bytes 8192 | tf_op jit(solution)/shard_map/all_to_all | solution.py:111
  148.9 31.2 %all-to-all-start.1 = ((bf16[8,4,131,128]{3,1,2,0:T(4,128)(2,1)}), bf16[8,4,131,128]{3,1,2,0:T(4,128)(2,1)S(1)}, u32[]{:S(2)}, u32[]{:S(2)}) async-start(bf16[8,4,131,128]{3,1,2,0:T(4,128)(2,1)} %copy.129), calls=%async_computation.1 | async-start | bytes 2146304 | tf_op jit(solution)/shard_map/all_to_all | solution.py:114
  155.7 26.2 %copy-start.1 = (bf16[128,1024]{1,0:T(8,128)(2,1)S(1)}, bf16[128,1024]{1,0:T(8,128)(2,1)}, u32[]{:S(2)}) copy-start(bf16[128,1024]{1,0:T(8,128)(2,1)} %param.23) | copy-start | bytes 786436
  155.7 26.2 %copy-start.11 = (f32[2,3,512]{2,0,1:T(2,128)S(1)}, f32[2,3,512]{2,0,1:T(2,128)}, u32[]{:S(2)}) copy-start(f32[2,3,512]{2,0,1:T(2,128)} %param.19) | copy-start | bytes 36868
  155.7 26.2 %copy-start.15 = (f32[128]{0:T(128)S(1)}, f32[128]{0:T(128)}, u32[]{:S(2)}) copy-start(f32[128]{0:T(128)} %param.25) | copy-start | bytes 1540
  155.7 26.2 %copy-start.24 = (bf16[128,128]{1,0:T(8,128)(2,1)S(1)}, bf16[128,128]{1,0:T(8,128)(2,1)}, u32[]{:S(2)}) copy-start(bf16[128,128]{1,0:T(8,128)(2,1)} %param.24) | copy-start | bytes 98308
  182.1 12.1 %copy-start.29 = (s32[2]{0:T(128)}, s32[2]{0:T(128)S(1)}, u32[]{:S(2)}) copy-start(s32[2]{0:T(128)S(1)} %get-tuple-element.660) | copy-start | bytes 28 | tf_op jit(solution)/shard_map/while
  194.2 5.2 %copy-start = (f32[8,128,512]{2,1,0:T(8,128)}, f32[8,128,512]{2,1,0:T(8,128)S(1)}, u32[]{:S(2)}) copy-start(f32[8,128,512]{2,1,0:T(8,128)S(1)} %get-tuple-element.583) | copy-start | bytes 6291460 | tf_op jit(solution)/shard_map/while
  194.2 5.2 %copy-start.31 = (f32[8]{0:T(128)}, f32[8]{0:T(128)S(1)}, u32[]{:S(2)}) copy-start(f32[8]{0:T(128)S(1)} %convert_multiply_fusion.5) | copy-start | bytes 100 | tf_op jit(solution)/shard_map/while
  209.9 7.0 %copy-start.16 = (f32[128]{0:T(128)S(1)}, f32[128]{0:T(128)}, u32[]{:S(2)}) copy-start(f32[128]{0:T(128)} %get-tuple-element.732) | copy-start | bytes 1540 | tf_op jit(solution)/shard_map/while
  209.9 7.0 %copy-start.25 = (bf16[128,128]{1,0:T(8,128)(2,1)S(1)}, bf16[128,128]{1,0:T(8,128)(2,1)}, u32[]{:S(2)}) copy-start(bf16[128,128]{1,0:T(8,128)(2,1)} %get-tuple-element.752) | copy-start | bytes 98308 | tf_op jit(solution)/shard_map/while
  209.9 7.0 %copy-start.27 = (f32[2,512]{1,0:T(2,128)S(1)}, f32[2,512]{1,0:T(2,128)}, u32[]{:S(2)}) copy-start(f32[2,512]{1,0:T(2,128)} %copy-done.26) | copy-start | bytes 12292 | tf_op jit(solution)/shard_map/while
  209.9 7.0 %copy-start.30 = (s32[2]{0:T(128)S(1)}, s32[2]{0:T(128)}, u32[]{:S(2)}) copy-start(s32[2]{0:T(128)} %copy-done.29) | copy-start | bytes 28 | tf_op jit(solution)/shard_map/while
  216.9 12.1 %copy-start.29 = (s32[2]{0:T(128)}, s32[2]{0:T(128)S(1)}, u32[]{:S(2)}) copy-start(s32[2]{0:T(128)S(1)} %get-tuple-element.660) | copy-start | bytes 28 | tf_op jit(solution)/shard_map/while
  229.0 5.2 %copy-start = (f32[8,128,512]{2,1,0:T(8,128)}, f32[8,128,512]{2,1,0:T(8,128)S(1)}, u32[]{:S(2)}) copy-start(f32[8,128,512]{2,1,0:T(8,128)S(1)} %get-tuple-element.583) | copy-start | bytes 6291460 | tf_op jit(solution)/shard_map/while
  229.0 5.2 %copy-start.31 = (f32[8]{0:T(128)}, f32[8]{0:T(128)S(1)}, u32[]{:S(2)}) copy-start(f32[8]{0:T(128)S(1)} %convert_multiply_fusion.5) | copy-start | bytes 100 | tf_op jit(solution)/shard_map/while
  244.7 7.0 %copy-start.16 = (f32[128]{0:T(128)S(1)}, f32[128]{0:T(128)}, u32[]{:S(2)}) copy-start(f32[128]{0:T(128)} %get-tuple-element.732) | copy-start | bytes 1540 | tf_op jit(solution)/shard_map/while
  244.7 7.0 %copy-start.25 = (bf16[128,128]{1,0:T(8,128)(2,1)S(1)}, bf16[128,128]{1,0:T(8,128)(2,1)}, u32[]{:S(2)}) copy-start(bf16[128,128]{1,0:T(8,128)(2,1)} %get-tuple-element.752) | copy-start | bytes 98308 | tf_op jit(solution)/shard_map/while
  244.7 7.0 %copy-start.27 = (f32[2,512]{1,0:T(2,128)S(1)}, f32[2,512]{1,0:T(2,128)}, u32[]{:S(2)}) copy-start(f32[2,512]{1,0:T(2,128)} %copy-done.26) | copy-start | bytes 12292 | tf_op jit(solution)/shard_map/while
  244.7 7.0 %copy-start.30 = (s32[2]{0:T(128)S(1)}, s32[2]{0:T(128)}, u32[]{:S(2)}) copy-start(s32[2]{0:T(128)} %copy-done.29) | copy-start | bytes 28 | tf_op jit(solution)/shard_map/while
  254.8 5.3 %copy-start.8 = (f32[2,128,1024]{2,1,0:T(8,128)S(1)}, f32[2,128,1024]{2,1,0:T(8,128)}, u32[]{:S(2)}) copy-start(f32[2,128,1024]{2,1,0:T(8,128)} %get-tuple-element.735) | copy-start | bytes 3145732
  256.3 29.5 %copy-start.14 = (f32[16,128]{1,0:T(8,128)S(1)}, f32[16,128]{1,0:T(8,128)}, u32[]{:S(2)}) copy-start(f32[16,128]{1,0:T(8,128)} %copy-done.13) | copy-start | bytes 24580
  256.3 29.5 %copy-start.23 = (f32[16,128,128]{2,0,1:T(8,128)S(1)}, f32[16,128,128]{2,0,1:T(8,128)}, u32[]{:S(2)}) copy-start(f32[16,128,128]{2,0,1:T(8,128)} %get-tuple-element.288) | copy-start | bytes 3145732
  256.3 29.5 %all-to-all-start.2 = ((bf16[8,4,128,128]{3,1,2,0:T(4,128)(2,1)}), bf16[8,4,128,128]{3,1,2,0:T(4,128)(2,1)S(1)}, u32[]{:S(2)}, u32[]{:S(2)}) async-start(bf16[8,4,128,128]{3,1,2,0:T(4,128)(2,1)} %copy.133), calls=%async_computation.2 | async-start | bytes 2097152 | tf_op jit(solution)/shard_map/all_to_all | solution.py:163
  260.0 109.7 %all-reduce.5.cloned.1.call-start = ((), (), s32[]{:S(2)}) async-start(), calls=%async_computation.3 | async-start | bytes 2228224 | tf_op jit(solution)/shard_map/psum | solution.py:180
  290.2 79.5 %copy-start.21 = (f32[2,128]{1,0:T(2,128)S(1)}, f32[2,128]{1,0:T(2,128)}, u32[]{:S(2)}) copy-start(f32[2,128]{1,0:T(2,128)} %get-tuple-element.737) | copy-start | bytes 3076
  290.3 118.4 %all-reduce.7.cloned.1.call-start = ((), (), s32[]{:S(2)}) async-start(), calls=%async_computation.4 | async-start | bytes 2228224 | tf_op jit(solution)/shard_map/psum | solution.py:189
  (21 other events, 41.7 us)
Sparse Core Ops, SparseCore 0:
  290.4 79.2 all-reduce.4
  372.2 36.4 all-reduce.6
